TPU v7x, 32 devices: a whole 2x2x4 slice. The times are simulated.
32 devices in a mesh: space: 8 (over z, y), ens: 4 (over x, core).
Axes of the slice: x: 2, y: 2, z: 4, core: 2. Of those that a mesh axis runs over, the one named last changes fastest.
Arguments:
- latent: bfloat16 [4, 6144, 1024], P('ens', 'space'), may hold values from -6 to 6
- head_weight: bfloat16 [1024, 100], replicated, may hold values from -0.1875 to 0.1875
- head_bias: float32 [100], replicated, may hold values from -3 to 3
- targets: bfloat16 [100, 6144], P(None, 'space'), may hold values from -6 to 6
- var_weight: float32 [100], replicated, may hold values from 0.25 to 2.5
- tile_fill: int32 [48], P('space'), may hold values from 1 to 128, 4608 in all
Outputs:
- grad_latent: bfloat16 [4, 6144, 1024], P('ens', 'space')
- grad_weight: float32 [1024, 100], replicated
- grad_bias: float32 [100], replicated
Inputs may be any that keep to these rules, and one draw needn't show every extreme that they name: tile_fill counts the live points of each tile.
All inputs are finite; a program needn't handle non-finite values. No bound on the sum of `tile_fill` on one device may be relied on, other than what follows from the above.
Results may differ from a plain program's by a relative error of at most 0.0099.
Values may be sent and summed in bfloat16 or wider, within the bound.
No kernel may reach another device: no remote copies, remote signals or barrier semaphores. Data moves between devices by JAX's collectives and lax.ppermute only.
A program may use at most 64 MiB of HBM per device.

v0:
```python
import jax
import jax.numpy as jnp
from jax import lax
from jax.sharding import PartitionSpec as P

TILE_PTS = 128
SMOOTH = 0.05


def smooth_sign(value):
    return value / jnp.sqrt(value * value + SMOOTH * SMOOTH)


def finish_grad(values, pair, area, observed, var_weight, members):
    grad = (
        area[None, None, :]
        * var_weight[None, :, None]
        * (smooth_sign(values - observed[None]) - pair / (members - 1))
    )
    return grad.astype(jnp.bfloat16)


def local(latent, head_weight, head_bias, targets, var_weight, tile_fill):
    mem_local = latent.shape[0]
    local_points = latent.shape[1]
    ens_count = lax.axis_size("ens")
    members = mem_local * ens_count
    points = local_points * lax.axis_size("space")
    preds = jnp.einsum("mpd,dv->mvp", latent, head_weight, preferred_element_type=jnp.float32)
    preds = (preds + head_bias[None, :, None]).astype(jnp.bfloat16)
    values = preds.astype(jnp.float32)
    local_index = jnp.arange(local_points, dtype=jnp.int32)
    global_index = lax.axis_index("space") * local_points + local_index
    fill = jnp.repeat(tile_fill, TILE_PTS)
    live = local_index % TILE_PTS < fill
    latitude = jnp.pi * ((global_index.astype(jnp.float32) + 0.5) / points - 0.5)
    area = jnp.where(live, jnp.cos(latitude), 0.0)
    observed = targets.astype(jnp.float32)
    piece = lax.all_gather(preds, "ens", axis=0, tiled=True)

    def one_member(slot, total):
        other = lax.dynamic_index_in_dim(piece, slot, 0, keepdims=True).astype(jnp.float32)
        return total + smooth_sign(values - other)

    pair = lax.fori_loop(0, piece.shape[0], one_member, jnp.zeros(values.shape, jnp.float32))
    grad_pred = finish_grad(values, pair, area, observed, var_weight, members)
    grad_latent = jnp.einsum(
        "mvp,dv->mpd", grad_pred, head_weight, preferred_element_type=jnp.float32
    ).astype(jnp.bfloat16)
    scale = 1.0 / jnp.sqrt(jnp.float32(members) * jnp.float32(points))
    weight_sum = (
        jnp.einsum("mpd,mvp->dv", latent, grad_pred, preferred_element_type=jnp.float32) * scale
    )
    bias_sum = jnp.sum(grad_pred.astype(jnp.float32), axis=(0, 2)) * scale
    weight_total, bias_total = lax.psum((weight_sum, bias_sum), ("space", "ens"))
    return (grad_latent, weight_total, bias_total)


def solution(mesh):
    placed = (P("ens", "space", None), P(), P(), P(None, "space"), P(), P("space"))
    return jax.shard_map(
        local,
        mesh=mesh,
        in_specs=placed,
        out_specs=(P("ens", "space", None), P(), P()),
        check_vma=False,
    )
```

profile of v0, /device:TPU:8, one launch (start us, length us, event | category | flops | bytes accessed | tf_op | source)
XLA Modules:
  0.0 157.8 jit_solution(4778582431813027777)
XLA Ops:
  7.2 0.0 copy-start
  7.2 0.0 all-reduce.2.cloned.1.call-start
  7.2 1.3 copy-done
  8.6 1.6 fusion.14
  10.2 7.8 %all-gather.1 = bf16[4,100,768]{2,1,0:T(8,128)(2,1)S(1)} all-gather(bf16[1,100,768]{2,1,0:T(8,128)(2,1)S(1)} %bitcast.38), channel_id=2, replica_groups=mesh['space'=8,'ens'=4] {'ens'}, dimensions={0}, use_global_device_ids=true | all-gather | bytes 768000 | tf_op jit(solution)/shard_map/all_gather | solution.py:39
  18.0 0.0 copy-start.4
  18.0 0.0 copy-start.2
  18.0 0.0 copy-start.3
  18.0 0.8 while.14
  18.0 0.2 select_add_fusion.2
  18.2 0.2 select_add_fusion.2
  18.4 0.2 select_add_fusion.2
  18.6 0.2 select_add_fusion.2
  18.8 0.0 copy-done.4
  18.8 0.1 cosine_select_fusion
  18.9 0.0 copy-done.2
  18.9 0.0 copy-done.3
  18.9 0.0 copy-start.1
  18.9 0.2 convert_reduce_fusion
  19.2 1.1 fusion.8
  20.3 0.0 all-reduce.2.cloned.1.call-update
  20.3 40.2 %psum.15 = f32[100]{0:T(128)} all-reduce(f32[100]{0:T(128)S(1)} %broadcast_multiply_fusion), channel_id=1, replica_groups=mesh['space'=8,'ens'=4] {'space','ens'}, use_global_device_ids=true, to_apply=%region_4.5 | all-reduce | flops 100 | bytes 800 | tf_op jit(solution)/shard_map/psum | solution.py:55
  60.6 0.0 copy-done.1
  60.6 1.8 %fusion.4 = bf16[1,768,1024]{2,1,0:T(8,128)(2,1)} fusion(bf16[1024,100]{0,1:T(8,128)(2,1)S(1)} %copy-done.1, bf16[1,100,768]{2,1,0:T(8,128)(2,1)S(1)} %get-tuple-element.107), kind=kOutput, calls=%fused_computation.6 | convolution fusion | flops 158072832 | bytes 1931264 | tf_op jit(solution)/shard_map/mvp,dv->mpd/dot_general | solution.py:47
  62.4 86.8 %all-reduce.2.cloned.1.call-done = f32[1024,100]{0,1:T(8,128)} async-done(((f32[1024,100]{0,1:T(8,128)}), f32[1024,100]{0,1:T(8,128)}) %all-reduce.2.cloned.1.call-update) | async-done | bytes 409616 | tf_op jit(solution)/shard_map/psum | solution.py:55
  149.2 1.8 %copy.16 = f32[1024,100]{0,1:T(8,128)} copy(f32[1024,100]{0,1:T(8,128)} %all-reduce.2.cloned.1.call-done) | data formatting | bytes 819200
  (3 shorter events, 0.0 us)
Async XLA Ops:
  7.2 1.4 copy-start
  7.2 142.0 %all-reduce.2.cloned.1.call-start = ((), (), s32[]{:S(2)}) async-start(), calls=%async_computation | async-start | bytes 851968 | tf_op jit(solution)/shard_map/psum | solution.py:55
  18.0 0.9 copy-start.4
  18.0 0.9 copy-start.2
  18.0 0.9 copy-start.3
  18.9 41.7 %copy-start.1 = (bf16[1024,100]{0,1:T(8,128)(2,1)S(1)}, bf16[1024,100]{0,1:T(8,128)(2,1)}, u32[]{:S(2)}) copy-start(bf16[1024,100]{0,1:T(8,128)(2,1)} %param.9) | copy-start | bytes 614404
Sparse Core Ops, SparseCore 0:
  20.5 128.6 all-reduce.1
where the time goes:
time: 158 us
  waiting for transfers between devices  86.8 us (55%)
  blocking collectives  48 us (30%)
  between operations  14.1 us (9%)
  matrix products  4.46 us (3%)
  local copies, waits for them, and re-layouts  3.15 us (2%)
    psum x1, waiting for transfers between devices, local(): lax.psum((weight_sum, bias_sum), ('space', 'ens'))  86.8 us
    psum x1, blocking collectives, local(): lax.psum((weight_sum, bias_sum), ('space', 'ens'))  40.2 us
    all_gather x1, blocking collectives, local(): piece = lax.all_gather(preds, 'ens', axis=0, tiled=True)  7.8 us
  transfers between devices with their start and end apart: 1, of which 1 were waited for; matrix products, arithmetic and copies ran while one was open for 1% of the time, Pallas kernels for 0%

commit v1 on v0

--- a/solution.py
+++ b/solution.py
@@ -5,6 +5,22 @@
 
 TILE_PTS = 128
 SMOOTH = 0.05
+
+
+def gather_around(x, axis, dim):
+    ways, here, step = (lax.axis_size(axis), lax.axis_index(axis), x.shape[dim])
+    lengths = [n * ways if d == dim else n for d, n in enumerate(x.shape)]
+    full = lax.dynamic_update_slice_in_dim(jnp.zeros(lengths, x.dtype), x, here * step, axis=dim)
+    going_up = going_down = x
+    for far in range(1, ways // 2 + 1):
+        going_up = lax.ppermute(going_up, axis, [(d, (d + 1) % ways) for d in range(ways)])
+        full = lax.dynamic_update_slice_in_dim(full, going_up, (here - far) % ways * step, axis=dim)
+        if 2 * far < ways:
+            going_down = lax.ppermute(going_down, axis, [(d, (d - 1) % ways) for d in range(ways)])
+            full = lax.dynamic_update_slice_in_dim(
+                full, going_down, (here + far) % ways * step, axis=dim
+            )
+    return full
 
 
 def smooth_sign(value):
@@ -36,7 +52,7 @@
     latitude = jnp.pi * ((global_index.astype(jnp.float32) + 0.5) / points - 0.5)
     area = jnp.where(live, jnp.cos(latitude), 0.0)
     observed = targets.astype(jnp.float32)
-    piece = lax.all_gather(preds, "ens", axis=0, tiled=True)
+    piece = gather_around(preds, "ens", 0)
 
     def one_member(slot, total):
         other = lax.dynamic_index_in_dim(piece, slot, 0, keepdims=True).astype(jnp.float32)

time: 158 us -> 161 us (1.019)
  waiting for transfers between devices: 86.8 us -> 94.2 us
  blocking collectives: 48 us -> 41.6 us
  starting transfers between devices: 0.04 us -> 1.86 us
    all_gather x1 -> x0, blocking collectives: 7.8 us -> none  [local(): piece = lax.all_gather(preds, 'ens', axis=0, tiled=True)]
    ppermute x0 -> x3, waiting for transfers between devices: none -> 7.41 us  [the longest x2 6.74 us: gather_around(): lax.ppermute(going_up, axis, [(d, (d + 1) % ways) for d in range(ways)])]
    ppermute x0 -> x3, starting transfers between devices: none -> 1.82 us  [the longest x1 1.73 us: gather_around(): lax.ppermute(going_down, axis, [(d, (d - 1) % ways) for d in range(ways)])]
  transfers between devices with their start and end apart: 1 -> 4, of which waited for: 1 -> 4; matrix products, arithmetic and copies ran while one was open for 1% -> 1% of each run, Pallas kernels for 0% -> 0%
where the time goes in v1:
time: 161 us
  waiting for transfers between devices  94.2 us (59%)
  blocking collectives  41.6 us (26%)
  between operations  14.2 us (9%)
  matrix products  4.46 us (3%)
  local copies, waits for them, and re-layouts  3.22 us (2%)
  starting transfers between devices  1.86 us (1%)
    psum x1, waiting for transfers between devices, local(): lax.psum((weight_sum, bias_sum), ('space', 'ens'))  86.8 us
    psum x1, blocking collectives, local(): lax.psum((weight_sum, bias_sum), ('space', 'ens'))  41.6 us
    ppermute x2, waiting for transfers between devices, gather_around(): lax.ppermute(going_up, axis, [(d, (d + 1) % ways) for d in range(ways)])  6.74 us
  transfers between devices with their start and end apart: 4, of which 4 were waited for; matrix products, arithmetic and copies ran while one was open for 1% of the time, Pallas kernels for 0%

profile of v1, /device:TPU:8, one launch (start us, length us, event | category | flops | bytes accessed | tf_op | source)
XLA Modules:
  0.0 160.7 jit_solution(13598980335350644561)
XLA Ops:
  7.2 0.0 copy-start
  7.2 0.0 all-reduce.2.cloned.1.call-start
  7.2 0.0 copy-start.4
  7.3 1.3 copy-done
  8.6 1.6 constant_dynamic-update-slice_fusion.3
  10.1 0.1 collective-permute-start
  10.2 1.7 %collective-permute-start.1 = (bf16[1,100,768]{2,1,0:T(8,128)(2,1)S(1)}, bf16[1,100,768]{2,1,0:T(8,128)(2,1)S(1)}, u32[]{:S(2)}, u32[]{:S(2)}) collective-permute-start(bf16[1,100,768]{2,1,0:T(8,128)(2,1)S(1)} %bitcast.42), channel_id=1, source_target_pairs={{0,3},{1,0},{2,1},{3,2},{4,7},{5,4},{6,5},{7,6},{8,11},{9,8},{10,9... | collective-permute-start | bytes 460808 | tf_op jit(solution)/shard_map/ppermute | solution.py:19
  12.0 0.0 copy-done.4
  12.0 0.1 cosine_select_fusion
  12.1 2.8 %collective-permute-done = bf16[1,100,768]{2,1,0:T(8,128)(2,1)S(1)} collective-permute-done((bf16[1,100,768]{2,1,0:T(8,128)(2,1)S(1)}, bf16[1,100,768]{2,1,0:T(8,128)(2,1)S(1)}, u32[]{:S(2)}, u32[]{:S(2)}) %collective-permute-start) | collective-permute-done | bytes 153632 | tf_op jit(solution)/shard_map/ppermute | solution.py:16
  14.9 0.0 collective-permute-start.2
  14.9 0.7 collective-permute-done.1
  15.6 4.0 %collective-permute-done.2 = bf16[1,100,768]{2,1,0:T(8,128)(2,1)S(1)} collective-permute-done((bf16[1,100,768]{2,1,0:T(8,128)(2,1)S(1)}, bf16[1,100,768]{2,1,0:T(8,128)(2,1)S(1)}, u32[]{:S(2)}, u32[]{:S(2)}) %collective-permute-start.2) | collective-permute-done | bytes 153632 | tf_op jit(solution)/shard_map/ppermute | solution.py:16
  19.6 0.0 copy-start.2
  19.6 0.0 copy-start.3
  19.6 0.9 while.14
  19.7 0.2 select_add_fusion.2
  19.9 0.2 select_add_fusion.2
  20.1 0.2 select_add_fusion.2
  20.3 0.2 select_add_fusion.2
  20.5 0.0 copy-done.2
  20.5 0.0 copy-done.3
  20.5 0.0 copy-start.1
  20.5 0.2 convert_reduce_fusion
  20.8 1.1 fusion.8
  21.9 0.0 all-reduce.2.cloned.1.call-update
  22.0 41.6 %psum.15 = f32[100]{0:T(128)} all-reduce(f32[100]{0:T(128)S(1)} %broadcast_multiply_fusion), channel_id=1, replica_groups=mesh['space'=8,'ens'=4] {'space','ens'}, use_global_device_ids=true, to_apply=%region_4.5 | all-reduce | flops 100 | bytes 800 | tf_op jit(solution)/shard_map/psum | solution.py:71
  63.5 0.0 copy-done.1
  63.5 1.8 %fusion.4 = bf16[1,768,1024]{2,1,0:T(8,128)(2,1)} fusion(bf16[1024,100]{0,1:T(8,128)(2,1)S(1)} %copy-done.1, bf16[1,100,768]{2,1,0:T(8,128)(2,1)S(1)} %get-tuple-element.107), kind=kOutput, calls=%fused_computation.6 | convolution fusion | flops 158072832 | bytes 1931264 | tf_op jit(solution)/shard_map/mvp,dv->mpd/dot_general | solution.py:63
  65.3 86.8 %all-reduce.2.cloned.1.call-done = f32[1024,100]{0,1:T(8,128)} async-done(((f32[1024,100]{0,1:T(8,128)}), f32[1024,100]{0,1:T(8,128)}) %all-reduce.2.cloned.1.call-update) | async-done | bytes 409616 | tf_op jit(solution)/shard_map/psum | solution.py:71
  152.1 1.8 %copy.20 = f32[1024,100]{0,1:T(8,128)} copy(f32[1024,100]{0,1:T(8,128)} %all-reduce.2.cloned.1.call-done) | data formatting | bytes 819200
  (7 shorter events, 0.1 us)
Async XLA Ops:
  7.2 1.4 copy-start
  7.2 144.9 %all-reduce.2.cloned.1.call-start = ((), (), s32[]{:S(2)}) async-start(), calls=%async_computation | async-start | bytes 851968 | tf_op jit(solution)/shard_map/psum | solution.py:71
  7.2 4.7 %copy-start.4 = (s32[6]{0:T(128)S(1)}, s32[6]{0:T(128)}, u32[]{:S(2)}) copy-start(s32[6]{0:T(128)} %param.13) | copy-start | bytes 76
  10.1 4.8 %collective-permute-start = (bf16[1,100,768]{2,1,0:T(8,128)(2,1)S(1)}, bf16[1,100,768]{2,1,0:T(8,128)(2,1)S(1)}, u32[]{:S(2)}, u32[]{:S(2)}) collective-permute-start(bf16[1,100,768]{2,1,0:T(8,128)(2,1)S(1)} %bitcast.41), channel_id=1, source_target_pairs={{0,1},{1,2},{2,3},{3,0},{4,5},{5,6},{6,7},{7,4},{8,9},{9,10},{10,1... | collective-permute-start | bytes 460808 | tf_op jit(solution)/shard_map/ppermute | solution.py:16
  10.2 5.4 %collective-permute-start.1 = (bf16[1,100,768]{2,1,0:T(8,128)(2,1)S(1)}, bf16[1,100,768]{2,1,0:T(8,128)(2,1)S(1)}, u32[]{:S(2)}, u32[]{:S(2)}) collective-permute-start(bf16[1,100,768]{2,1,0:T(8,128)(2,1)S(1)} %bitcast.42), channel_id=1, source_target_pairs={{0,3},{1,0},{2,1},{3,2},{4,7},{5,4},{6,5},{7,6},{8,11},{9,8},{10,9... | collective-permute-start | bytes 460808 | tf_op jit(solution)/shard_map/ppermute | solution.py:19
  14.9 4.7 %collective-permute-start.2 = (bf16[1,100,768]{2,1,0:T(8,128)(2,1)S(1)}, bf16[1,100,768]{2,1,0:T(8,128)(2,1)S(1)}, u32[]{:S(2)}, u32[]{:S(2)}) collective-permute-start(bf16[1,100,768]{2,1,0:T(8,128)(2,1)S(1)} %collective-permute-done), channel_id=1, source_target_pairs={{0,1},{1,2},{2,3},{3,0},{4,5},{5,6},{6,7},{7,4},{8,9},{9,10},{10,1... | collective-permute-start | bytes 460808 | tf_op jit(solution)/shard_map/ppermute | solution.py:16
  19.6 0.9 copy-start.2
  19.6 0.9 copy-start.3
  20.5 43.0 %copy-start.1 = (bf16[1024,100]{0,1:T(8,128)(2,1)S(1)}, bf16[1024,100]{0,1:T(8,128)(2,1)}, u32[]{:S(2)}) copy-start(bf16[1024,100]{0,1:T(8,128)(2,1)} %param.9) | copy-start | bytes 614404
Sparse Core Ops, SparseCore 0:
  22.1 129.9 all-reduce.1
